TPU v7x, 128 devices: a whole 4x4x4 slice. The times are simulated.
128 devices in a mesh: grp: 8 (over z, core), ep: 16 (over x, y).
Axes of the slice: x: 4, y: 4, z: 4, core: 2. Of those that a mesh axis runs over, the one named last changes fastest.
Arguments:
- hidden_in: bfloat16 [16384, 2048], P(('grp', 'ep')), may hold values from -24 to 24
- prompt_lengths: int32 [8, 5], P('grp'), may hold values from 1 to 1024, 2048 in all within a row
- routes: int32 [16384, 6], P(('grp', 'ep')), may hold values from 0 to 63, all different within a row; in each aligned block of 128 rows (0 to 127, 128 to 255, ...) at most 16 rows name the same one
- route_weights: float32 [16384, 6], P(('grp', 'ep')), may hold values from 0.05 to 0.4
- w_query: bfloat16 [2048, 2048], P(None, 'ep'), may hold values from -3 to 3
- w_key: bfloat16 [2048, 2048], P(None, 'ep'), may hold values from -3 to 3
- w_value: bfloat16 [2048, 2048], P(None, 'ep'), may hold values from -0.125 to 0.125
- w_out: bfloat16 [2048, 2048], replicated, may hold values from -0.125 to 0.125
- shared_gate: bfloat16 [2048, 2816], P(None, 'grp'), may hold values from -0.125 to 0.125
- shared_up: bfloat16 [2048, 2816], P(None, 'grp'), may hold values from -0.125 to 0.125
- shared_down: bfloat16 [2816, 2048], P('grp'), may hold values from -0.109375 to 0.109375
- expert_gate: bfloat16 [128, 2048, 704], P(('grp', 'ep')), may hold values from -0.125 to 0.125
- expert_up: bfloat16 [128, 2048, 704], P(('grp', 'ep')), may hold values from -0.125 to 0.125
- expert_down: bfloat16 [128, 704, 2048], P(('grp', 'ep')), may hold values from -0.15625 to 0.15625
Outputs:
- attended: bfloat16 [16384, 2048], P(('grp', 'ep'))
- moe_update: bfloat16 [16384, 2048], P(('grp', 'ep'))
Inputs may be any that keep to these rules, and one draw needn't show every extreme that they name: `routes`: each row names 6 different experts. The 128 rows of one device name any one expert at most 16 times, and in every draw some device names some expert exactly 16 times. `prompt_lengths`: row g describes group g: its first 4 entries are the lengths of the packed prompts in order, the last one the padding positions at the group's end. Each row sums to 2048, and its largest entry is 1024.
All inputs are finite; a program needn't handle non-finite values.
Results may differ from a plain program's by a relative error of at most 0.015.
The roundings to bfloat16 on the way count: a program that leaves them out, or rounds other values in their place, can miss the bound.
Values may be sent and summed in bfloat16 or wider, within the bound.
A program may use at most 128 MiB of HBM per device.

v0:
```python
import math

import jax
import jax.numpy as jnp
from jax import lax
from jax.sharding import PartitionSpec as P

HDIM = 128


epsilon = 1e-06


def rms_rows(values):
    mean_square = jnp.mean(values * values, axis=-1, keepdims=True)
    return values * lax.rsqrt(mean_square + epsilon)


def segment_ids(length_row, row_total):
    prompt_ends = jnp.cumsum(length_row[:-1])
    positions = jnp.arange(row_total, dtype=jnp.int32)
    segment = jnp.sum((positions[:, None] >= prompt_ends[None, :]).astype(jnp.int32), axis=1)
    return jnp.where(segment >= length_row.shape[0] - 1, -1, segment)


def attend(queries, key_rows, value_rows, segment, block_rows):
    row_total, heads_here, head_dim = queries.shape
    score_scale = 1.0 / math.sqrt(head_dim)
    positions = jnp.arange(row_total, dtype=jnp.int32)

    def one_block(first_row):
        query_block = lax.dynamic_slice_in_dim(queries, first_row, block_rows, 0)
        query_pos = first_row + jnp.arange(block_rows, dtype=jnp.int32)
        query_seg = lax.dynamic_slice_in_dim(segment, first_row, block_rows, 0)
        scores = (
            jnp.einsum("qhd,khd->hqk", query_block, key_rows, preferred_element_type=jnp.float32)
            * score_scale
        )
        allowed = (
            (positions[None, :] <= query_pos[:, None])
            & (segment[None, :] == query_seg[:, None])
            & ((query_seg[:, None] >= 0) | (positions[None, :] == query_pos[:, None]))
        )
        scores = jnp.where(allowed[None], scores, -1e30)
        largest = jnp.max(scores, axis=2, keepdims=True)
        weights = jnp.where(allowed[None], jnp.exp(scores - largest), 0.0)
        totals = jnp.sum(weights, axis=2, keepdims=True)
        attn_probs = (weights / totals).astype(jnp.bfloat16)
        mixed_rows = jnp.einsum(
            "hqk,khd->qhd", attn_probs, value_rows, preferred_element_type=jnp.float32
        )
        return mixed_rows.astype(jnp.bfloat16)

    starts = jnp.arange(row_total // block_rows, dtype=jnp.int32) * block_rows
    blocks = lax.map(one_block, starts)
    return blocks.reshape(row_total, heads_here * head_dim)


def expert_rows(received, gate_half, up_half, down_half):
    width = received.shape[2]
    flattened = received.reshape(-1, width)
    gate_act = jnp.dot(flattened, gate_half, preferred_element_type=jnp.float32)
    up_act = jnp.dot(flattened, up_half, preferred_element_type=jnp.float32)
    hidden = (jax.nn.silu(gate_act) * up_act).astype(jnp.bfloat16)
    partial_value = jnp.dot(hidden, down_half, preferred_element_type=jnp.float32).astype(
        jnp.bfloat16
    )
    return partial_value.reshape(received.shape)


def local(
    hidden_in,
    prompt_lengths,
    routes,
    route_weights,
    w_query,
    w_key,
    w_value,
    w_out,
    shared_gate,
    shared_up,
    shared_down,
    expert_gate,
    expert_up,
    expert_down,
):
    tok_rows, width = hidden_in.shape
    top_count = routes.shape[1]
    grp_count = lax.axis_size("grp")
    ep_count = lax.axis_size("ep")
    device_count = grp_count * ep_count
    expert_count = device_count // 2
    capacity = 8 * tok_rows // expert_count
    group_rows = tok_rows * ep_count
    local_width = w_query.shape[1]
    heads_here = local_width // HDIM
    normed = rms_rows(hidden_in.astype(jnp.float32)).astype(jnp.bfloat16)
    w_joined = jnp.concatenate((w_query, w_key, w_value), axis=1)
    joined = jnp.dot(
        lax.all_gather(normed, "ep", axis=0, tiled=True),
        w_joined,
        preferred_element_type=jnp.float32,
    ).astype(jnp.bfloat16)
    queries = joined[:, :local_width].reshape(group_rows, heads_here, HDIM)
    key_rows = joined[:, local_width : 2 * local_width].reshape(group_rows, heads_here, HDIM)
    value_rows = joined[:, 2 * local_width :].reshape(group_rows, heads_here, HDIM)
    segment = segment_ids(prompt_lengths[0], group_rows)
    heads_local = attend(queries, key_rows, value_rows, segment, min(512, group_rows))
    heads_out = lax.all_to_all(heads_local, "ep", split_axis=0, concat_axis=1, tiled=True)
    residual = hidden_in.astype(jnp.float32) + jnp.dot(
        heads_out, w_out, preferred_element_type=jnp.float32
    )
    normed_moe = rms_rows(residual).astype(jnp.bfloat16)
    gathered = lax.all_gather(normed_moe, "grp", axis=0, tiled=True)
    gate_act = jnp.dot(gathered, shared_gate, preferred_element_type=jnp.float32)
    up_act = jnp.dot(gathered, shared_up, preferred_element_type=jnp.float32)
    hidden = (jax.nn.silu(gate_act) * up_act).astype(jnp.bfloat16)
    shared_out = lax.psum_scatter(
        jnp.dot(hidden, shared_down, preferred_element_type=jnp.float32).astype(jnp.bfloat16),
        "grp",
        scatter_dimension=0,
        tiled=True,
    ).astype(jnp.float32)
    flat_experts = routes.reshape(-1)
    route_total = flat_experts.shape[0]
    onehot = (flat_experts[:, None] == jnp.arange(expert_count, dtype=jnp.int32)[None, :]).astype(
        jnp.int32
    )
    rank_in = jnp.sum((jnp.cumsum(onehot, axis=0) - onehot) * onehot, axis=1)
    slot_index = flat_experts * capacity + rank_in
    token_index = jnp.arange(route_total, dtype=jnp.int32) // top_count
    slot_source = (
        jnp.full((expert_count * capacity,), tok_rows, jnp.int32).at[slot_index].set(token_index)
    )
    padded_rows = jnp.concatenate((normed_moe, jnp.zeros((1, width), jnp.bfloat16)), axis=0)
    outbound = padded_rows[slot_source].reshape(expert_count, 1, capacity, width)
    outbound = jnp.broadcast_to(outbound, (expert_count, 2, capacity, width)).reshape(
        device_count, capacity, width
    )
    gate_half = expert_gate[0]
    up_half = expert_up[0]
    down_half = expert_down[0]
    returned = lax.all_to_all(
        expert_rows(
            lax.all_to_all(outbound, ("grp", "ep"), split_axis=0, concat_axis=0, tiled=True),
            gate_half,
            up_half,
            down_half,
        ),
        ("grp", "ep"),
        split_axis=0,
        concat_axis=0,
        tiled=True,
    )
    by_expert = returned.reshape(expert_count, 2, capacity, width)
    first_half = by_expert[flat_experts, 0, rank_in]
    second_half = by_expert[flat_experts, 1, rank_in]
    expert_sum = first_half.astype(jnp.float32) + second_half.astype(jnp.float32)
    weighted = expert_sum * route_weights.reshape(-1, 1)
    routed = jnp.sum(weighted.reshape(tok_rows, top_count, width), axis=1)
    attended = residual.astype(jnp.bfloat16)
    moe_update = (shared_out + routed).astype(jnp.bfloat16)
    return (attended, moe_update)


def solution(mesh):
    in_specs = (
        P(("grp", "ep"), None),
        P("grp", None),
        P(("grp", "ep"), None),
        P(("grp", "ep"), None),
        P(None, "ep"),
        P(None, "ep"),
        P(None, "ep"),
        P(),
        P(None, "grp"),
        P(None, "grp"),
        P("grp", None),
        P(("grp", "ep"), None, None),
        P(("grp", "ep"), None, None),
        P(("grp", "ep"), None, None),
    )
    out_specs = (P(("grp", "ep"), None), P(("grp", "ep"), None))
    return jax.shard_map(local, mesh=mesh, in_specs=in_specs, out_specs=out_specs, check_vma=False)
```

profile of v0, /device:TPU:4, one launch (start us, length us, event | category | flops | bytes accessed | tf_op | source)
XLA Modules:
  0.0 497.3 jit_solution(996202673333153389)
XLA Ops:
  14.6 69.1 %all-gather.3.cloned.1.call-done = bf16[2048,2048]{1,0:T(8,128)(2,1)} async-done(((bf16[128,2048]{1,0:T(8,128)(2,1)}), bf16[2048,2048]{1,0:T(8,128)(2,1)}) %all-gather.3.cloned.1.call-update) | async-done | bytes 8388624 | tf_op jit(solution)/shard_map/all_gather | solution.py:100
  83.8 8.3 %convolution_convert_fusion.2 = bf16[2048,384]{1,0:T(8,128)(2,1)S(1)} fusion(bf16[2048,2048]{1,0:T(8,128)(2,1)} %all-gather.3.cloned.1.call-done, bf16[2048,128]{1,0:T(8,128)(2,1)} %param.22, bf16[2048,128]{1,0:T(8,128)(2,1)} %param.21, bf16[2048,128]{1,0:T(8,128)(2,1)} %param.20), kind=kOutput, calls=%fused_computation.40 | convolution fusion | flops 3226730496 | bytes 11534336 | tf_op jit(solution)/shard_map/dot_general | solution.py:99
  93.3 53.6 %while.12 = (s32[]{:T(128)}, bf16[4,512,1,128]{3,1,2,0:T(8,128)(2,1)}, s32[4]{0:T(128)S(1)}, s32[2048]{0:T(1024)S(1)}, bf16[2048,1,128]{2,0,1:T(8,128)(2,1)}, /*...) while((s32[]{:T(128)}, ...), condition=%wide.region_6.7_spmd.clone.clone, body=%wide.region_3.6_spmd.clone.clone.sunk | while | flops 570490880 | bytes 16046279 | solution.py:55
  96.8 3.3 fusion.70
  100.1 2.9 fusion.71
  103.0 3.7 fusion.72
  110.2 3.3 fusion.70
  113.6 2.9 fusion.71
  116.4 3.7 fusion.72
  123.7 3.3 fusion.70
  129.8 3.7 fusion.72
  137.1 3.3 fusion.70
  143.2 3.7 fusion.72
  146.9 6.0 %all-to-all-start = ((bf16[16,128,128]{2,1,0:T(8,128)(2,1)}), bf16[16,128,128]{2,1,0:T(8,128)(2,1)}, u32[]{:S(2)}, u32[]{:S(2)}) async-start(bf16[16,128,128]{2,1,0:T(8,128)(2,1)} %bitcast.95), calls=%async_computation | async-start | bytes 1048576 | tf_op jit(solution)/shard_map/all_to_all | solution.py:109
  154.4 3.4 scatter_custom_fusion
  157.8 4.1 all-to-all-done
  163.9 4.9 multiply_reduce_fusion.1
  171.1 6.0 %gather_fusion = bf16[1024,2048]{1,0:T(8,128)(2,1)} fusion(bf16[129,2048]{1,0:T(8,128)(2,1)S(1)} %concatenate.13, s32[1024]{0:T(1024)S(1)} %fusion.42), kind=kCustom, calls=%fused_computation | custom fusion | bytes 8392704 | tf_op jit(solution)/shard_map/gather | solution.py:136
  177.1 6.7 %broadcast_in_dim.43 = bf16[64,2,16,2048]{3,2,1,0:T(8,128)(2,1)} broadcast(bf16[64,16,2048]{2,1,0:T(8,128)(2,1)} %bitcast.92), dimensions={0,2,3} | broadcast | bytes 12582912 | tf_op jit(solution)/shard_map/broadcast_in_dim | solution.py:137
  183.9 8.5 %all-to-all-start.1 = ((bf16[128,16,2048]{2,1,0:T(8,128)(2,1)}), bf16[128,16,2048]{2,1,0:T(8,128)(2,1)}, u32[]{:S(2)}, u32[]{:S(2)}) async-start(bf16[128,16,2048]{2,1,0:T(8,128)(2,1)} %bitcast.91), calls=%async_computation.2 | async-start | bytes 16777216 | tf_op jit(solution)/shard_map/all_to_all | solution.py:145
  193.1 101.7 %all-to-all-done.1 = bf16[128,16,2048]{2,1,0:T(8,128)(2,1)} async-done(((bf16[128,16,2048]{2,1,0:T(8,128)(2,1)}), bf16[128,16,2048]{2,1,0:T(8,128)(2,1)}, u32[]{:S(2)}, u32[]{:S(2)}) %all-to-all-start.1) | async-done | bytes 8388640 | tf_op jit(solution)/shard_map/all_to_all | solution.py:145
  294.8 11.1 %fusion.24 = f32[2048,704]{0,1:T(8,128)} fusion(bf16[2048,2048]{1,0:T(8,128)(2,1)} %bitcast.11, bf16[1,2048,704]{1,2,0:T(8,128)(2,1)} %param.27), kind=kOutput, calls=%fused_computation.37 | convolution fusion | flops 5905580032 | bytes 17039360 | tf_op jit(solution)/shard_map/dot_general | solution.py:62
  305.9 19.1 %convolution_convert_fusion = bf16[2048,2048]{1,0:T(8,128)(2,1)} fusion(f32[2048,704]{0,1:T(8,128)} %fusion.24, bf16[2048,2048]{1,0:T(8,128)(2,1)} %bitcast.11, bf16[1,704,2048]{2,1,0:T(8,128)(2,1)S(1)} %copy-done, bf16[1,2048,704]{1,2,0:T(8,128)(2,1)} %param.28), kind=kOutput, calls=%fused_computation.31 | convolution fusion | flops 11824005120 | bytes 28311552 | tf_op jit(solution)/shard_map/dot_general | solution.py:65
  324.9 7.3 %all-to-all-start.2 = ((bf16[128,16,2048]{2,1,0:T(8,128)(2,1)}), bf16[128,16,2048]{2,1,0:T(8,128)(2,1)}, u32[]{:S(2)}, u32[]{:S(2)}) async-start(bf16[128,16,2048]{2,1,0:T(8,128)(2,1)} %bitcast.93), calls=%async_computation.3 | async-start | bytes 16777216 | tf_op jit(solution)/shard_map/all_to_all | solution.py:143
  332.5 5.4 %fusion.54 = f32[1024,352]{0,1:T(8,128)} fusion(bf16[1024,2048]{1,0:T(8,128)(2,1)} %all-gather.5.cloned.1.call-done, bf16[2048,352]{0,1:T(8,128)(2,1)} %param.24), kind=kOutput, calls=%fused_computation.100 | convolution fusion | flops 1476395008 | bytes 7077888 | tf_op jit(solution)/shard_map/dot_general | solution.py:115
  337.9 9.4 %convolution_convert_fusion.1 = bf16[1024,2048]{1,0:T(8,128)(2,1)} fusion(bf16[352,2048]{1,0:T(8,128)(2,1)} %param.26, bf16[1024,2048]{1,0:T(8,128)(2,1)} %all-gather.5.cloned.1.call-done, bf16[2048,352]{0,1:T(8,128)(2,1)} %param.25, f32[1024,352]{0,1:T(8,128)} %fusion.54), kind=kOutput, calls=%fused_computation.34 | convolution fusion | flops 2957049856 | bytes 12713984 | tf_op jit(solution)/shard_map/dot_general | solution.py:119
  348.1 86.7 %all-to-all-done.2 = bf16[128,16,2048]{2,1,0:T(8,128)(2,1)} async-done(((bf16[128,16,2048]{2,1,0:T(8,128)(2,1)}), bf16[128,16,2048]{2,1,0:T(8,128)(2,1)}, u32[]{:S(2)}, u32[]{:S(2)}) %all-to-all-start.2) | async-done | bytes 8388640 | tf_op jit(solution)/shard_map/all_to_all | solution.py:143
  434.8 15.4 %gather_fusion.2 = bf16[768,2048]{1,0:T(8,128)(2,1)} fusion(bf16[64,2,16,2048]{3,2,1,0:T(8,128)(2,1)} %bitcast.16, s32[768]{0:T(1024)S(1)} %get-tuple-element.92), kind=kCustom, calls=%fused_computation.2 | custom fusion | bytes 6300672 | tf_op jit(solution)/shard_map/gather | solution.py:157
  450.2 15.5 %gather_fusion.1 = bf16[768,2048]{1,0:T(8,128)(2,1)} fusion(bf16[64,2,16,2048]{3,2,1,0:T(8,128)(2,1)} %bitcast.16, s32[768]{0:T(1024)S(1)} %get-tuple-element.91), kind=kCustom, calls=%fused_computation.1 | custom fusion | bytes 6300672 | tf_op jit(solution)/shard_map/gather | solution.py:156
  465.7 6.9 %convert_add_fusion = f32[768,2048]{1,0:T(8,128)} fusion(bf16[768,2048]{1,0:T(8,128)(2,1)} %gather_fusion.2, bf16[768,2048]{1,0:T(8,128)(2,1)} %gather_fusion.1), kind=kLoop, calls=%fused_computation.32 | loop fusion | flops 4718592 | bytes 12582912 | tf_op jit(solution)/shard_map/add | solution.py:158
  472.6 7.8 %add.123 = f32[128,6,2048]{2,1,0:T(8,128)} reshape(f32[768,2048]{1,0:T(8,128)} %convert_add_fusion) | data formatting | bytes 12582912 | tf_op jit(solution)/shard_map/add | solution.py:158
  480.5 7.6 %multiply_reduce_fusion = f32[128,2048]{1,0:T(8,128)} fusion(f32[128,6,2048]{2,1,0:T(8,128)} %add.123, f32[128,6]{1,0:T(8,128)S(1)} %copy.36), kind=kLoop, calls=%fused_computation.30 | loop fusion | flops 2883584 | bytes 7343104 | tf_op jit(solution)/shard_map/reduce_sum | solution.py:160
  (66 shorter events, 29.9 us)
Async XLA Ops:
  7.2 298.7 %copy-start = (bf16[1,704,2048]{2,1,0:T(8,128)(2,1)S(1)}, bf16[1,704,2048]{2,1,0:T(8,128)(2,1)}, u32[]{:S(2)}) copy-start(bf16[1,704,2048]{2,1,0:T(8,128)(2,1)} %param.29) | copy-start | bytes 8650756
  7.2 76.6 %all-gather.3.cloned.1.call-start = ((), (), s32[]{:S(2)}) async-start(), calls=%async_computation.4 | async-start | bytes 8912896 | tf_op jit(solution)/shard_map/all_gather | solution.py:100
  14.2 77.8 %copy-start.2 = (s32[64,6,128]{2,0,1:T(8,128)}, s32[64,6,128]{2,0,1:T(8,128)S(1)}, u32[]{:S(2)}) copy-start(s32[64,6,128]{2,0,1:T(8,128)S(1)} %reduce-window.19) | copy-start | bytes 589828
  93.3 70.6 %copy-start.1 = (bf16[128,2048]{1,0:T(8,128)(2,1)S(1)}, bf16[128,2048]{1,0:T(8,128)(2,1)}, u32[]{:S(2)}) copy-start(bf16[128,2048]{1,0:T(8,128)(2,1)} %param.16) | copy-start | bytes 1572868
  100.1 2.9 copy-start.3
  113.5 2.9 copy-start.3
  126.9 2.9 copy-start.3
  140.4 2.9 copy-start.3
  146.9 15.0 %all-to-all-start = ((bf16[16,128,128]{2,1,0:T(8,128)(2,1)}), bf16[16,128,128]{2,1,0:T(8,128)(2,1)}, u32[]{:S(2)}, u32[]{:S(2)}) async-start(bf16[16,128,128]{2,1,0:T(8,128)(2,1)} %bitcast.95), calls=%async_computation | async-start | bytes 1048576 | tf_op jit(solution)/shard_map/all_to_all | solution.py:109
  183.9 110.9 %all-to-all-start.1 = ((bf16[128,16,2048]{2,1,0:T(8,128)(2,1)}), bf16[128,16,2048]{2,1,0:T(8,128)(2,1)}, u32[]{:S(2)}, u32[]{:S(2)}) async-start(bf16[128,16,2048]{2,1,0:T(8,128)(2,1)} %bitcast.91), calls=%async_computation.2 | async-start | bytes 16777216 | tf_op jit(solution)/shard_map/all_to_all | solution.py:145
  192.3 140.2 %all-gather.5.cloned.1.call-start = ((), (), s32[]{:S(2)}) async-start(), calls=%async_computation.5 | async-start | bytes 4718592 | tf_op jit(solution)/shard_map/all_gather | solution.py:114
  324.9 109.9 %all-to-all-start.2 = ((bf16[128,16,2048]{2,1,0:T(8,128)(2,1)}), bf16[128,16,2048]{2,1,0:T(8,128)(2,1)}, u32[]{:S(2)}, u32[]{:S(2)}) async-start(bf16[128,16,2048]{2,1,0:T(8,128)(2,1)} %bitcast.93), calls=%async_computation.3 | async-start | bytes 16777216 | tf_op jit(solution)/shard_map/all_to_all | solution.py:143
  332.2 155.9 %reduce-scatter.2.cloned.1.call-start = ((), (), s32[]{:S(2)}) async-start(), calls=%async_computation.6 | async-start | bytes 4718592 | tf_op jit(solution)/shard_map/reduce_scatter | solution.py:118
  347.3 0.7 copy-start.4
Sparse Core Ops, SparseCore 0:
  10.8 72.9 all-gather.2
  195.4 108.5 all-gather.4
  347.4 101.5 reduce-scatter.1
where the time goes:
time: 507 us; the launch traced here: 497 us
  waiting for transfers between devices  262 us (52%)
  matrix products  86.1 us (17%)
  local copies, waits for them, and re-layouts  64.8 us (13%)
  other arithmetic  39.1 us (8%)
  starting transfers between devices  22.1 us (4%)
  between operations  14.3 us (3%)
  loops' own time  8.41 us (2%)
    all_to_all x1, waiting for transfers between devices, local(): lax.all_to_all(outbound, ('grp', 'ep'), split_axis=0, concat_axis=0, tile...  102 us
    all_to_all x1, waiting for transfers between devices, local(): lax.all_to_all(expert_rows(lax.all_to_all(outbound, ('grp', 'ep'), split_...  86.7 us
    all_gather x1, waiting for transfers between devices, local(): lax.all_gather(normed, 'ep', axis=0, tiled=True)  69.1 us
    dot_general x1, matrix products, expert_rows(): jnp.dot(hidden, down_half, preferred_element_type=jnp.float32)  19.1 us
    gather x1, local copies, waits for them, and re-layouts, local(): first_half = by_expert[flat_experts, 0, rank_in]  15.5 us
    gather x1, local copies, waits for them, and re-layouts, local(): second_half = by_expert[flat_experts, 1, rank_in]  15.4 us
    dot_general x4, matrix products, one_block(): jnp.einsum('hqk,khd->qhd', attn_probs, value_rows, preferred_element_type...  14.8 us
    dot_general x4, matrix products, one_block(): jnp.einsum('qhd,khd->hqk', query_block, key_rows, preferred_element_type=...  13.2 us
  transfers between devices with their start and end apart: 6, of which 4 were waited for; matrix products, arithmetic and copies ran while one was open for 22% of the time, Pallas kernels for 0%

commit v1 on v0

v1 whole, which is shorter than its diff:
```python
import math

import jax
import jax.numpy as jnp
from jax import lax
from jax.experimental import pallas as pl
from jax.experimental.pallas import tpu as pltpu
from jax.sharding import PartitionSpec as P

MESH = pl.DeviceIdType.MESH
HDIM = 128
EPS = 1e-06
SIDE = 4
F32 = jnp.float32
BF16 = jnp.bfloat16


def nt_dot(a, b):
    return lax.dot_general(a, b, (((1,), (1,)), ((), ())), preferred_element_type=F32)


def nn_dot(a, b):
    return jnp.dot(a, b, preferred_element_type=F32)


def front_kernel(
    lens, hid, wq, wk, wv, wo_hbm, att_out, nm_out,
    g, w, wo, qkv, o, h, res, w_sem, ss, rs, hs, hr,
):
    tok, width = hid.shape
    half_w = width // 2
    ep_count = SIDE * SIDE
    rows_all = tok * ep_count
    grp = lax.axis_index("grp")
    me = lax.axis_index("ep")
    x = me // SIDE
    y = lax.rem(me, SIDE)

    w_copies = [
        pltpu.make_async_copy(src, w.at[:, pl.ds(n * HDIM, HDIM)], w_sem.at[n])
        for n, src in enumerate((wq, wk, wv))
    ]
    w_copies.append(pltpu.make_async_copy(wo_hbm, wo, w_sem.at[3]))
    for c in w_copies:
        c.start()

    barrier = pltpu.get_barrier_semaphore()

    @pl.loop(1, ep_count)
    def _(k):
        pl.semaphore_signal(
            barrier, inc=1, device_id=(grp, lax.rem(me + k, ep_count)), device_id_type=MESH
        )

    hv = hid[...].astype(F32)
    scale = lax.rsqrt(jnp.mean(hv * hv, axis=-1, keepdims=True) + EPS)
    normed = (hv * scale).astype(BF16)
    own_rows = pl.ds(pl.multiple_of(me * tok, tok), tok)
    g[0, own_rows, :] = normed[:, :half_w]
    g[1, own_rows, :] = normed[:, half_w:]
    pl.semaphore_wait(barrier, ep_count - 1)

    sends = []

    def region(half, dx, dy, piece):
        src = lax.rem(x + dx, SIDE) * SIDE + lax.rem(y + dy, SIDE)
        if piece is None:
            return g.at[half, pl.ds(pl.multiple_of(src * tok, tok), tok), :]
        sub = tok // 2
        return g.at[half, pl.ds(pl.multiple_of(src * tok + sub * piece, sub), sub), :]

    def coords(half, p, q):
        return (p, q) if half == 0 else (q, p)

    def send(half, p, q, piece, first_axis, sign):
        dx, dy = coords(half, p, q)
        rp, rq = ((p - sign) % SIDE, q) if first_axis else (p, (q - sign) % SIDE)
        rdx, rdy = coords(half, rp, rq)
        along_x = first_axis == (half == 0)
        step = sign % SIDE
        if along_x:
            dest = lax.rem(x + step, SIDE) * SIDE + y
        else:
            dest = x * SIDE + lax.rem(y + step, SIDE)
        ref = region(half, dx, dy, piece)
        d = pltpu.make_async_remote_copy(
            src_ref=ref,
            dst_ref=ref,
            send_sem=ss.at[len(sends)],
            recv_sem=rs.at[half, rdx, rdy, piece or 0],
            device_id=(grp, dest),
            device_id_type=MESH,
        )
        d.start()
        sends.append(d)

    def arrive(half, p, q, piece=None):
        dx, dy = coords(half, p, q)
        ref = region(half, dx, dy, piece)
        pltpu.make_async_remote_copy(
            src_ref=ref,
            dst_ref=ref,
            send_sem=ss.at[0],
            recv_sem=rs.at[half, dx, dy, piece or 0],
            device_id=(grp, lax.rem(me + 1, ep_count)),
            device_id_type=MESH,
        ).wait_recv()

    both = (0, 1)

    def fan(half, p):
        for sign in (1, -1):
            send(half, p, 0, None, False, sign)

    for half in both:
        for sign in (1, -1):
            send(half, 0, 0, None, True, sign)
    for half in both:
        fan(half, 0)
    for half in both:
        arrive(half, 3, 0)
        send(half, 3, 0, 0, True, 1)
        arrive(half, 1, 0)
        send(half, 1, 0, 1, True, -1)
    for half in both:
        fan(half, 3)
        fan(half, 1)

    def pass_on(half, p):
        arrive(half, p, 3)
        send(half, p, 3, 0, False, 1)
        arrive(half, p, 1)
        send(half, p, 1, 1, False, -1)

    for half in both:
        pass_on(half, 0)
    for half in both:
        arrive(half, 2, 0, 0)
        arrive(half, 2, 0, 1)
        fan(half, 2)
    for half in both:
        pass_on(half, 3)
        pass_on(half, 1)

    for c in w_copies[:3]:
        c.wait()

    def project(dx):
        start = pl.multiple_of(lax.rem(x + dx, SIDE) * (SIDE * tok), SIDE * tok)
        rows = pl.ds(start, SIDE * tok)
        acc = nn_dot(g[0, rows, :], w[:half_w, :]) + nn_dot(g[1, rows, :], w[half_w:, :])
        qkv[rows, :] = acc.astype(BF16)

    arrive(0, 0, 2, 0)
    arrive(0, 0, 2, 1)
    for half in both:
        pass_on(half, 2)
    project(0)
    for dx in (3, 1):
        arrive(0, dx, 2, 0)
        arrive(0, dx, 2, 1)
        project(dx)
    for piece in both:
        arrive(0, 2, 2, piece)
        for dy in range(SIDE):
            arrive(1, dy, 2, piece)
    project(2)

    ends = [lens[0, 0]]
    for j in range(1, 4):
        ends.append(ends[-1] + lens[0, j])
    q_rows = 2 * tok
    big = SIDE * tok
    score_scale = 1.0 / math.sqrt(HDIM)
    head_sends = []
    for i in range(SIDE):
        keys = (i + 1) * big

        @pl.loop(0, big // q_rows)
        def _(r):
            row0 = pl.multiple_of(i * big + r * q_rows, q_rows)
            qb = qkv[pl.ds(row0, q_rows), :HDIM]
            s = nt_dot(qb, qkv[:keys, HDIM : 2 * HDIM]) * score_scale
            pos = row0 + lax.broadcasted_iota(jnp.int32, (q_rows, 1), 0)
            first = jnp.zeros_like(pos)
            for e in ends[:3]:
                first = jnp.where(pos >= e, e, first)
            first = jnp.where(pos >= ends[3], pos, first)
            kpos = lax.broadcasted_iota(jnp.int32, (q_rows, keys), 1)
            s = jnp.where((kpos >= first) & (kpos <= pos), s, -1e30)
            e = jnp.exp(s - jnp.max(s, axis=1, keepdims=True))
            inv = 1.0 / jnp.sum(e, axis=1, keepdims=True)
            probs = (e * inv).astype(BF16)
            o[pl.ds(row0, q_rows), :] = nn_dot(probs, qkv[:keys, 2 * HDIM :]).astype(BF16)

        for j in range(SIDE * i, SIDE * i + SIDE):
            d = pltpu.make_async_remote_copy(
                src_ref=o.at[pl.ds(j * tok, tok), :],
                dst_ref=h.at[:, pl.ds(pl.multiple_of(me * HDIM, HDIM), HDIM)],
                send_sem=hs.at[j],
                recv_sem=hr.at[me],
                device_id=(grp, j),
                device_id_type=MESH,
            )
            head_sends.append(d)

            @pl.when(me != j)
            def _():
                d.start()

    h[:, pl.ds(pl.multiple_of(me * HDIM, HDIM), HDIM)] = o[own_rows, :]
    for d in sends:
        d.wait_send()
    w_copies[3].wait()
    for j in range(ep_count):
        d = pltpu.make_async_remote_copy(
            src_ref=o.at[pl.ds(j * tok, tok), :],
            dst_ref=h.at[:, pl.ds(j * HDIM, HDIM)],
            send_sem=hs.at[j],
            recv_sem=hr.at[j],
            device_id=(grp, j),
            device_id_type=MESH,
        )

        @pl.when(me != j)
        def _():
            d.wait_send()
            d.wait_recv()

    total = jnp.zeros((tok, 1), F32)
    chunk = width // 4
    for c in range(4):
        cols = slice(c * chunk, (c + 1) * chunk)
        part = hid[:, cols].astype(F32) + nn_dot(h[...], wo[:, cols])
        res[:, cols] = part
        total = total + jnp.sum(part * part, axis=1, keepdims=True)
    scale2 = lax.rsqrt(total / width + EPS)
    att_out[...] = res[...].astype(BF16)
    nm_out[...] = (res[...] * scale2).astype(BF16)


def front(hidden_in, prompt_lengths, w_query, w_key, w_value, w_out):
    tok, width = hidden_in.shape
    rows_all = tok * SIDE * SIDE
    any_spec = pl.BlockSpec(memory_space=pl.ANY)
    vmem = pl.BlockSpec(memory_space=pltpu.VMEM)
    out = jax.ShapeDtypeStruct((tok, width), BF16)
    return pl.pallas_call(
        front_kernel,
        out_shape=(out, out),
        in_specs=[pl.BlockSpec(memory_space=pltpu.SMEM), vmem] + [any_spec] * 4,
        out_specs=(vmem, vmem),
        scratch_shapes=[
            pltpu.VMEM((2, rows_all, width // 2), BF16),
            pltpu.VMEM((width, 3 * HDIM), BF16),
            pltpu.VMEM((width, width), BF16),
            pltpu.VMEM((rows_all, 3 * HDIM), BF16),
            pltpu.VMEM((rows_all, HDIM), BF16),
            pltpu.VMEM((tok, width), BF16),
            pltpu.VMEM((tok, width), F32),
            pltpu.SemaphoreType.DMA((4,)),
            pltpu.SemaphoreType.DMA((40,)),
            pltpu.SemaphoreType.DMA((2, SIDE, SIDE, 2)),
            pltpu.SemaphoreType.DMA((SIDE * SIDE,)),
            pltpu.SemaphoreType.DMA((SIDE * SIDE,)),
        ],
        compiler_params=pltpu.CompilerParams(collective_id=0, has_side_effects=True),
        name="front",
    )(prompt_lengths, hidden_in, w_query, w_key, w_value, w_out)


def slot_matrix(routes_t, weights_t, expert_count, capacity):
    tok = routes_t.shape[1]
    experts = jnp.arange(expert_count, dtype=jnp.int32)
    hit = routes_t[:, None, :] == experts[None, :, None]
    mask = jnp.any(hit, axis=0)
    gate = jnp.sum(jnp.where(hit, weights_t[:, None, :], 0.0), axis=0)
    earlier = jnp.arange(tok)[:, None] < jnp.arange(tok)[None, :]
    rank = nn_dot(mask.astype(BF16), earlier.astype(BF16)).astype(jnp.int32)
    rank = jnp.where(mask, rank, -1)
    pick = rank[:, None, :] == jnp.arange(capacity, dtype=jnp.int32)[None, :, None]
    pick = pick.reshape(expert_count * capacity, tok)
    gates = jnp.broadcast_to(gate[:, None, :], (expert_count, capacity, tok)).reshape(pick.shape)
    return pick.astype(BF16), jnp.where(pick, gates, 0.0)


def local(
    hidden_in, prompt_lengths, routes, route_weights, w_query, w_key, w_value, w_out,
    shared_gate, shared_up, shared_down, expert_gate, expert_up, expert_down,
):
    tok_rows, width = hidden_in.shape
    device_count = lax.axis_size("grp") * lax.axis_size("ep")
    expert_count = device_count // 2
    capacity = 8 * tok_rows // expert_count
    pick, gates = slot_matrix(routes.T, route_weights.T, expert_count, capacity)
    attended, normed_moe = front(hidden_in, prompt_lengths, w_query, w_key, w_value, w_out)

    gathered = lax.all_gather(normed_moe, "grp", axis=0, tiled=True)
    gate_act = nn_dot(gathered, shared_gate)
    up_act = nn_dot(gathered, shared_up)
    hidden = (jax.nn.silu(gate_act) * up_act).astype(BF16)
    shared_out = lax.psum_scatter(
        nn_dot(hidden, shared_down).astype(BF16), "grp", scatter_dimension=0, tiled=True
    ).astype(F32)

    outbound = nn_dot(pick, normed_moe).astype(BF16).reshape(expert_count, 1, capacity, width)
    outbound = jnp.broadcast_to(outbound, (expert_count, 2, capacity, width)).reshape(
        device_count, capacity, width
    )
    received = lax.all_to_all(outbound, ("grp", "ep"), split_axis=0, concat_axis=0, tiled=True)
    flat = received.reshape(-1, width)
    act = jax.nn.silu(nn_dot(flat, expert_gate[0])) * nn_dot(flat, expert_up[0])
    parts = nn_dot(act.astype(BF16), expert_down[0]).astype(BF16).reshape(received.shape)
    returned = lax.all_to_all(parts, ("grp", "ep"), split_axis=0, concat_axis=0, tiled=True)
    both = jnp.broadcast_to(
        gates.reshape(expert_count, 1, capacity, tok_rows),
        (expert_count, 2, capacity, tok_rows),
    ).reshape(device_count * capacity, tok_rows)
    high = both.astype(BF16)
    low = (both - high.astype(F32)).astype(BF16)
    mix = jnp.concatenate((high, low), axis=1)
    sums = lax.dot_general(
        mix, returned.reshape(-1, width), (((0,), (0,)), ((), ())), preferred_element_type=F32
    )
    routed = sums[:tok_rows] + sums[tok_rows:]
    return attended, (shared_out + routed).astype(BF16)


def solution(mesh):
    in_specs = (
        P(("grp", "ep"), None),
        P("grp", None),
        P(("grp", "ep"), None),
        P(("grp", "ep"), None),
        P(None, "ep"),
        P(None, "ep"),
        P(None, "ep"),
        P(),
        P(None, "grp"),
        P(None, "grp"),
        P("grp", None),
        P(("grp", "ep"), None, None),
        P(("grp", "ep"), None, None),
        P(("grp", "ep"), None, None),
    )
    out_specs = (P(("grp", "ep"), None), P(("grp", "ep"), None))
    return jax.shard_map(local, mesh=mesh, in_specs=in_specs, out_specs=out_specs, check_vma=False)
```

time: 507 us -> 386 us (0.76); the launches traced: 497 us -> 382 us
  Pallas kernels: 0 us -> 66.5 us
  local copies, waits for them, and re-layouts: 64.8 us -> 9.17 us
  waiting for transfers between devices: 262 us -> 210 us
  other arithmetic: 39.1 us -> 3.82 us
  matrix products: 86.1 us -> 56.1 us
  loops' own time: 8.41 us -> 0 us
    all_gather x1, waiting for transfers between devices: 0.02 us -> 111 us  [local(): gathered = lax.all_gather(normed_moe, 'grp', axis=0, tiled=True)]
    all_to_all x1, waiting for transfers between devices: 102 us -> 0.01 us  [local(): lax.all_to_all(outbound, ('grp', 'ep'), split_axis=0, concat_axis=0, tile...]
    all_gather x1 -> x0, waiting for transfers between devices: 69.1 us -> none  [local(): lax.all_gather(normed, 'ep', axis=0, tiled=True)]
    pallas_call x0 -> x1, Pallas kernels: none -> 66.5 us  [front(): pl.pallas_call(front_kernel, out_shape=(out, out), in_specs=[pl.BlockSpec...]
    gather x3 -> x0, local copies, waits for them, and re-layouts: 36.9 us -> none  [the longest x1 15.5 us: local(): first_half = by_expert[flat_experts, 0, rank_in]]
    dot_general x14 -> x7, matrix products: 86.1 us -> 56.1 us  [the longest x6 48.5 us: nn_dot(): return jnp.dot(a, b, preferred_element_type=F32)]
    reduce_sum x8 -> x1, other arithmetic: 21.6 us -> 0.03 us  [slot_matrix(): gate = jnp.sum(jnp.where(hit, weights_t[:, None, :], 0.0), axis=0)]
    add x5 -> x0, other arithmetic: 9.67 us -> none  [the longest x1 6.9 us: local(): first_half.astype(jnp.float32) + second_half.astype(jnp.float32)]
  transfers between devices with their start and end apart: 6 -> 4, of which waited for: 4 -> 3; matrix products, arithmetic and copies ran while one was open for 22% -> 6% of each run, Pallas kernels for 0% -> 0%
where the time goes in v1:
time: 386 us; the launch traced here: 382 us
  waiting for transfers between devices  210 us (54%)
  Pallas kernels  66.5 us (17%)
  matrix products  56.1 us (15%)
  starting transfers between devices  22.9 us (6%)
  between operations  14.1 us (4%)
  local copies, waits for them, and re-layouts  9.17 us (2%)
    all_gather x1, waiting for transfers between devices, local(): gathered = lax.all_gather(normed_moe, 'grp', axis=0, tiled=True)  111 us
    all_to_all x1, waiting for transfers between devices, local(): lax.all_to_all(parts, ('grp', 'ep'), split_axis=0, concat_axis=0, tiled=T...  92.1 us
    pallas_call x1, Pallas kernels, front(): pl.pallas_call(front_kernel, out_shape=(out, out), in_specs=[pl.BlockSpec...  66.5 us
    dot_general x6, matrix products, nn_dot(): return jnp.dot(a, b, preferred_element_type=F32)  48.5 us
    all_to_all x1, starting transfers between devices, local(): lax.all_to_all(outbound, ('grp', 'ep'), split_axis=0, concat_axis=0, tile...  14.2 us
    all_to_all x1, starting transfers between devices, local(): lax.all_to_all(parts, ('grp', 'ep'), split_axis=0, concat_axis=0, tiled=T...  8.41 us
  transfers between devices with their start and end apart: 4, of which 3 were waited for; matrix products, arithmetic and copies ran while one was open for 6% of the time, Pallas kernels for 0%

profile of v1, /device:TPU:4, one launch (start us, length us, event | category | flops | bytes accessed | tf_op | source)
XLA Modules:
  0.0 382.4 jit_solution(6197420344103800964)
XLA Ops:
  7.2 0.0 copy-start
  7.2 0.1 eq.49
  7.3 0.9 fusion.17
  8.1 0.1 fusion.7
  8.3 0.2 bitcast_compare_fusion
  8.5 66.5 %front.1 = (bf16[128,2048]{1,0:T(8,128)(2,1)}, bf16[128,2048]{1,0:T(8,128)(2,1)}) custom-call(s32[1,5]{1,0:T(1,128)} %lens.1, bf16[128,2048]{1,0:T(8,128)(2,1)} %hid.1, bf16[2048,128]{1,0:T(8,128)(2,1)} %wq.1, bf16[2048,128]{1,0:T(8,128)(2,1)} %wk.1, bf16[2048,128]{1,0:T(8,128)(2,1)} %wv.1, bf16[2048,2048]{1,0:T(8,128)(2,1)} %wo_hbm.1), custom_call_target="tpu_custom_call" | custom-call | tf_op jit(solution)/shard_map/front/pallas_call | solution.py:248
  75.0 4.3 %convolution_convert_fusion.2 = bf16[1024,2048]{1,0:T(8,128)(2,1)} fusion(pred[1024,128]{1,0:T(32,128)(4,1)S(1)} %bitcast_compare_fusion, bf16[128,2048]{1,0:T(8,128)(2,1)} %get-tuple-element.5), kind=kOutput, calls=%fused_computation.3 | convolution fusion | flops 538968064 | bytes 4849664 | tf_op jit(solution)/shard_map/dot_general | solution.py:23
  79.3 6.8 %broadcast_in_dim.52 = bf16[64,2,16,2048]{3,2,1,0:T(8,128)(2,1)} broadcast(bf16[64,16,2048]{2,1,0:T(8,128)(2,1)} %bitcast.38), dimensions={0,2,3} | broadcast | bytes 12582912 | tf_op jit(solution)/shard_map/broadcast_in_dim | solution.py:307
  86.1 14.2 %all-to-all-start = ((bf16[128,16,2048]{2,1,0:T(8,128)(2,1)}), bf16[128,16,2048]{2,1,0:T(8,128)(2,1)}, u32[]{:S(2)}, u32[]{:S(2)}) async-start(bf16[128,16,2048]{2,1,0:T(8,128)(2,1)} %bitcast.37), calls=%async_computation.1 | async-start | bytes 16777216 | tf_op jit(solution)/shard_map/all_to_all | solution.py:310
  100.2 0.0 all-gather.2.cloned.1.call-start
  100.3 0.7 all-gather.2.cloned.1.call-update
  101.0 110.9 %all-gather.2.cloned.1.call-done = bf16[1024,2048]{1,0:T(8,128)(2,1)} async-done(((bf16[128,2048]{1,0:T(8,128)(2,1)}), bf16[1024,2048]{1,0:T(8,128)(2,1)}) %all-gather.2.cloned.1.call-update) | async-done | bytes 4194320 | tf_op jit(solution)/shard_map/all_gather | solution.py:298
  211.9 5.4 %fusion.21 = f32[1024,352]{0,1:T(8,128)} fusion(bf16[1024,2048]{1,0:T(8,128)(2,1)} %all-gather.2.cloned.1.call-done, bf16[2048,352]{0,1:T(8,128)(2,1)} %param.22), kind=kOutput, calls=%fused_computation.34 | convolution fusion | flops 1476395008 | bytes 7077888 | tf_op jit(solution)/shard_map/dot_general | solution.py:23
  217.3 0.0 all-to-all-done
  217.3 11.0 %fusion.3 = f32[2048,704]{0,1:T(8,128)} fusion(bf16[2048,2048]{1,0:T(8,128)(2,1)} %bitcast.6, bf16[1,2048,704]{1,2,0:T(8,128)(2,1)} %param.25), kind=kOutput, calls=%fused_computation.6 | convolution fusion | flops 5905580032 | bytes 17039360 | tf_op jit(solution)/shard_map/dot_general | solution.py:23
  228.4 0.0 copy-done
  228.4 19.1 %convolution_convert_fusion = bf16[2048,2048]{1,0:T(8,128)(2,1)} fusion(f32[2048,704]{0,1:T(8,128)} %fusion.3, bf16[2048,2048]{1,0:T(8,128)(2,1)} %bitcast.6, bf16[1,704,2048]{2,1,0:T(8,128)(2,1)S(1)} %copy-done, bf16[1,2048,704]{1,2,0:T(8,128)(2,1)} %param.26), kind=kOutput, calls=%fused_computation | convolution fusion | flops 11824005120 | bytes 28311552 | tf_op jit(solution)/shard_map/dot_general | solution.py:23
  247.5 8.4 %all-to-all-start.1 = ((bf16[128,16,2048]{2,1,0:T(8,128)(2,1)}), bf16[128,16,2048]{2,1,0:T(8,128)(2,1)}, u32[]{:S(2)}, u32[]{:S(2)}) async-start(bf16[128,16,2048]{2,1,0:T(8,128)(2,1)} %bitcast.39), calls=%async_computation.2 | async-start | bytes 16777216 | tf_op jit(solution)/shard_map/all_to_all | solution.py:314
  255.9 0.3 reduce-scatter.2.cloned.1.call-start
  256.2 0.0 copy-done.5
  256.2 0.0 copy-done.6
  256.2 8.6 %convolution_convert_fusion.1 = bf16[1024,2048]{1,0:T(8,128)(2,1)} fusion(bf16[352,2048]{1,0:T(8,128)(2,1)S(1)} %copy-done.5, bf16[1024,2048]{1,0:T(8,128)(2,1)} %all-gather.2.cloned.1.call-done, bf16[2048,352]{0,1:T(8,128)(2,1)S(1)} %copy-done.6, f32[1024,352]{0,1:T(8,128)} %fusion.21), kind=kOutput, calls=%fused_computation.2 | convolution fusion | flops 2957049856 | bytes 12713984 | tf_op jit(solution)/shard_map/dot_general | solution.py:23
  264.7 0.0 reduce-scatter.2.cloned.1.call-update
  264.8 0.7 copy-done.3
  265.4 0.0 copy-done.4
  265.6 0.8 bitcast_convert_fusion
  266.4 92.1 %all-to-all-done.1 = bf16[128,16,2048]{2,1,0:T(8,128)(2,1)} async-done(((bf16[128,16,2048]{2,1,0:T(8,128)(2,1)}), bf16[128,16,2048]{2,1,0:T(8,128)(2,1)}, u32[]{:S(2)}, u32[]{:S(2)}) %all-to-all-start.1) | async-done | bytes 8388640 | tf_op jit(solution)/shard_map/all_to_all | solution.py:314
  358.5 7.6 %fusion.11 = f32[256,2048]{1,0:T(8,128)} fusion(bf16[2048,2048]{1,0:T(8,128)(2,1)} %bitcast.11, bf16[2048,128]{1,0:T(8,128)(2,1)S(1)} %fusion.8, bf16[2048,128]{1,0:T(8,128)(2,1)} %bitcast_convert_fusion), kind=kOutput, calls=%fused_computation.19 | convolution fusion | flops 2149580800 | bytes 11534336 | tf_op jit(solution)/shard_map/dot_general | solution.py:322
  366.1 6.0 %reduce-scatter.2.cloned.1.call-done = bf16[128,2048]{1,0:T(8,128)(2,1)} async-done(((bf16[1024,2048]{1,0:T(8,128)(2,1)}), bf16[128,2048]{1,0:T(8,128)(2,1)}) %reduce-scatter.2.cloned.1.call-update) | async-done | bytes 524304 | tf_op jit(solution)/shard_map/reduce_scatter | solution.py:302
  372.1 2.6 fusion.10
  374.8 0.0 copy-done.2
  374.8 0.8 copy.19
  (11 shorter events, 0.1 us)
Async XLA Ops:
  7.2 221.2 %copy-start = (bf16[1,704,2048]{2,1,0:T(8,128)(2,1)S(1)}, bf16[1,704,2048]{2,1,0:T(8,128)(2,1)}, u32[]{:S(2)}) copy-start(bf16[1,704,2048]{2,1,0:T(8,128)(2,1)} %param.27) | copy-start | bytes 8650756
  86.1 131.3 %all-to-all-start = ((bf16[128,16,2048]{2,1,0:T(8,128)(2,1)}), bf16[128,16,2048]{2,1,0:T(8,128)(2,1)}, u32[]{:S(2)}, u32[]{:S(2)}) async-start(bf16[128,16,2048]{2,1,0:T(8,128)(2,1)} %bitcast.37), calls=%async_computation.1 | async-start | bytes 16777216 | tf_op jit(solution)/shard_map/all_to_all | solution.py:310
  100.2 111.7 %all-gather.2.cloned.1.call-start = ((), (), s32[]{:S(2)}) async-start(), calls=%async_computation.3 | async-start | bytes 4718592 | tf_op jit(solution)/shard_map/all_gather | solution.py:298
  247.5 8.7 %copy-start.5 = (bf16[352,2048]{1,0:T(8,128)(2,1)S(1)}, bf16[352,2048]{1,0:T(8,128)(2,1)}, u32[]{:S(2)}) copy-start(bf16[352,2048]{1,0:T(8,128)(2,1)} %param.24) | copy-start | bytes 4325380
  247.5 8.7 %copy-start.6 = (bf16[2048,352]{0,1:T(8,128)(2,1)S(1)}, bf16[2048,352]{0,1:T(8,128)(2,1)}, u32[]{:S(2)}) copy-start(bf16[2048,352]{0,1:T(8,128)(2,1)} %param.23) | copy-start | bytes 4325380
  247.5 111.1 %all-to-all-start.1 = ((bf16[128,16,2048]{2,1,0:T(8,128)(2,1)}), bf16[128,16,2048]{2,1,0:T(8,128)(2,1)}, u32[]{:S(2)}, u32[]{:S(2)}) async-start(bf16[128,16,2048]{2,1,0:T(8,128)(2,1)} %bitcast.39), calls=%async_computation.2 | async-start | bytes 16777216 | tf_op jit(solution)/shard_map/all_to_all | solution.py:314
  255.9 116.2 %reduce-scatter.2.cloned.1.call-start = ((), (), s32[]{:S(2)}) async-start(), calls=%async_computation.4 | async-start | bytes 4718592 | tf_op jit(solution)/shard_map/reduce_scatter | solution.py:302
  264.7 0.7 copy-start.3
  264.7 0.7 copy-start.4
  358.5 17.0 %copy-start.1 = (bf16[1,704,2048]{2,1,0:T(8,128)(2,1)S(1)}, bf16[1,704,2048]{2,1,0:T(8,128)(2,1)}, u32[]{:S(2)}) copy-start(bf16[1,704,2048]{2,1,0:T(8,128)(2,1)} %param.27) | copy-start | bytes 8650756
  366.1 8.7 %copy-start.2 = (bf16[128,2048]{1,0:T(8,128)(2,1)S(1)}, bf16[128,2048]{1,0:T(8,128)(2,1)}, u32[]{:S(2)}) copy-start(bf16[128,2048]{1,0:T(8,128)(2,1)} %get-tuple-element.8) | copy-start | bytes 1572868
Sparse Core Ops, SparseCore 0:
  102.8 109.1 all-gather.1
  264.9 107.2 reduce-scatter.1
